TPU v7x, 32 devices: a whole 2x2x4 slice. The times are simulated.
32 devices in a mesh: kt: 4 (over z), ks: 8 (over y, x, core).
Axes of the slice: x: 2, y: 2, z: 4, core: 2. Of those that a mesh axis runs over, the one named last changes fastest.
Arguments:
- val_target: bfloat16 [8, 32, 512], P('kt', None, 'ks'), may hold values from -6 to 6
- cond_target: bfloat16 [8, 64, 512], P('kt', None, 'ks'), may hold values from -0.046875 to 0.046875
- val_source: bfloat16 [32, 32, 512], P('ks', None, 'kt'), may hold values from -6 to 6
- cond_source: bfloat16 [32, 64, 512], P('ks', None, 'kt'), may hold values from -0.125 to 0.125
- trial_vectors: bfloat16 [32, 16, 2048], P('ks', 'kt'), may hold values from -6 to 6
- screened: bfloat16 [512, 512, 512], P(None, ('kt', 'ks')), may hold values from -0.25 to 0.25
- pair_momentum: int32 [8, 32], replicated, may hold values from 0 to 511
Outputs:
- kernel_out: float32 [8, 16, 2048], P('kt', 'ks')
All inputs are finite; a program needn't handle non-finite values.
Results may differ from a plain program's by a relative error of at most 0.019.
Values may be sent and summed in bfloat16 or wider, within the bound.
A program may use at most 128 MiB of HBM per device.

v0:
```python
import jax
import jax.numpy as jnp
from jax import lax
from jax.sharding import PartitionSpec as P


def local(val_target, cond_target, val_source, cond_source, trial_vectors, screened, pair_momentum):
    tgt_val, tgt_cond = (
        lax.all_gather(val_target, "ks", axis=2, tiled=True),
        lax.all_gather(cond_target, "ks", axis=2, tiled=True),
    )
    src_val, src_cond, vectors = (
        lax.all_gather(val_source, "kt", axis=2, tiled=True),
        lax.all_gather(cond_source, "kt", axis=2, tiled=True),
        lax.all_gather(trial_vectors, "kt", axis=1, tiled=True),
    )
    count_kt = lax.axis_size("kt")
    count_ks = lax.axis_size("ks")
    tgt_count = tgt_val.shape[0]
    src_count = src_val.shape[0]
    pair_count = tgt_count * src_count
    width = screened.shape[2]
    val_bands = tgt_val.shape[1]
    cond_bands = tgt_cond.shape[1]
    vec_count = vectors.shape[1]
    table = pair_momentum.reshape(count_kt, tgt_count, count_ks, src_count)
    table = table.transpose(1, 3, 0, 2).reshape(pair_count, count_kt * count_ks)
    outgoing = screened[table]
    arrived = lax.all_to_all(outgoing, ("kt", "ks"), split_axis=1, concat_axis=1, tiled=True)
    pair_mats = arrived.reshape(tgt_count, src_count, width, width)
    trial_four = vectors.reshape(src_count, vec_count, val_bands, cond_bands)
    dressed = jnp.einsum(
        "snwc,scq->snwq", trial_four, src_cond, preferred_element_type=jnp.float32
    ).astype(jnp.bfloat16)
    pair_prod = (
        tgt_val.astype(jnp.float32)[:, None, :, None, :]
        * src_val.astype(jnp.float32)[None, :, None, :, :]
    ).astype(jnp.bfloat16)
    kernels = jnp.einsum(
        "tsvwp,tspq->tsvwq", pair_prod, pair_mats, preferred_element_type=jnp.float32
    ).astype(jnp.bfloat16)
    reduced = jnp.einsum(
        "tsvwq,snwq->tvnq", kernels, dressed, preferred_element_type=jnp.float32
    ).astype(jnp.bfloat16)
    partial_out = jnp.einsum(
        "tvnq,tcq->tnvc", reduced, tgt_cond, preferred_element_type=jnp.float32
    )
    partial_out = partial_out.reshape(tgt_count, vec_count, val_bands * cond_bands)
    return lax.psum_scatter(
        partial_out.astype(jnp.bfloat16), "ks", scatter_dimension=1, tiled=True
    ).astype(jnp.float32)


def solution(mesh):
    in_specs = (
        P("kt", None, "ks"),
        P("kt", None, "ks"),
        P("ks", None, "kt"),
        P("ks", None, "kt"),
        P("ks", "kt", None),
        P(None, ("kt", "ks"), None),
        P(),
    )
    out_specs = P("kt", "ks", None)
    return jax.shard_map(local, mesh=mesh, in_specs=in_specs, out_specs=out_specs, check_vma=False)
```

profile of v0, /device:TPU:0, one launch (start us, length us, event | category | flops | bytes accessed | tf_op | source)
XLA Modules:
  0.0 324.3 jit_solution(9907673848661414223)
XLA Ops:
  6.5 0.8 reshape.45
  7.3 0.1 copy.39
  7.4 0.1 reshape.46
  7.5 0.1 reshape.50
  7.6 6.2 %gather_fusion = bf16[256,16,512]{2,1,0:T(8,128)(2,1)} fusion(bf16[512,16,512]{2,1,0:T(8,128)(2,1)} %param.12, s32[1024]{0:T(1024)S(1)} %pad_clamp_fusion), kind=kCustom, calls=%fused_computation | custom fusion | bytes 8389632 | tf_op jit(solution)/shard_map/gather | solution.py:28
  13.8 0.0 copy-start.4
  13.8 0.0 copy-start.2
  13.8 0.0 copy-start.1
  13.8 0.0 copy-start
  13.8 4.8 %copy.40 = bf16[8,32,16,512]{3,2,0,1:T(8,128)(2,1)} copy(bf16[8,32,16,512]{3,2,1,0:T(8,128)(2,1)} %bitcast.36) | data formatting | bytes 8388608 | tf_op jit(solution)/shard_map/gather | solution.py:28
  18.6 7.5 %all-to-all-start = ((bf16[8,32,16,512]{3,2,0,1:T(8,128)(2,1)}), bf16[8,32,16,512]{3,2,0,1:T(8,128)(2,1)}, u32[]{:S(2)}, u32[]{:S(2)}) async-start(bf16[8,32,16,512]{3,2,0,1:T(8,128)(2,1)} %copy.40), calls=%async_computation | async-start | bytes 8388608 | tf_op jit(solution)/shard_map/all_to_all | solution.py:29
  26.1 0.0 all-reduce.3.cloned.1.call-start
  26.1 0.0 copy-done.4
  26.1 0.1 copy.37
  26.2 0.0 copy-start.3
  26.2 33.5 %all_gather.17 = bf16[2,32,512]{1,0,2:T(2,128)(2,1)S(1)} all-gather(bf16[2,32,64]{1,0,2:T(2,128)(2,1)S(1)} %copy.37), channel_id=1, replica_groups=mesh['kt'=4,'ks'=8] {'ks'}, dimensions={2}, use_global_device_ids=true | all-gather | bytes 73728 | tf_op jit(solution)/shard_map/all_gather | solution.py:9
  59.8 0.1 copy.38
  59.9 0.0 copy-done.2
  59.9 66.6 %all_gather.18 = bf16[4,32,512]{2,1,0:T(8,128)(2,1)S(1)} all-gather(bf16[4,32,128]{2,1,0:T(8,128)(2,1)S(1)} %copy-done.2), channel_id=1, replica_groups=mesh['kt'=4,'ks'=8] {'kt'}, dimensions={2}, use_global_device_ids=true | all-gather | bytes 163840 | tf_op jit(solution)/shard_map/all_gather | solution.py:13
  126.6 0.0 copy-done.1
  126.6 0.1 copy.35
  126.7 13.9 %all_gather.15 = bf16[4,16,2048]{2,0,1:T(4,128)(2,1)S(1)} all-gather(bf16[4,4,2048]{2,0,1:T(4,128)(2,1)S(1)} %copy.35), channel_id=1, replica_groups=mesh['kt'=4,'ks'=8] {'kt'}, dimensions={1}, use_global_device_ids=true | all-gather | bytes 327680 | tf_op jit(solution)/shard_map/all_gather | solution.py:15
  140.5 0.1 copy.36
  140.7 0.5 reshape.44
  141.2 0.0 copy-done
  141.2 12.8 %all_gather.16 = bf16[4,64,512]{2,1,0:T(8,128)(2,1)S(1)} all-gather(bf16[4,64,128]{2,1,0:T(8,128)(2,1)S(1)} %copy-done), channel_id=1, replica_groups=mesh['kt'=4,'ks'=8] {'kt'}, dimensions={2}, use_global_device_ids=true | all-gather | bytes 327680 | tf_op jit(solution)/shard_map/all_gather | solution.py:14
  154.1 0.7 convert_bitcast_fusion
  154.8 12.0 %copy.50 = bf16[4,16,32,512,1]{2,1,0,4,3:T(8,128)(2,1)} copy(bf16[4,16,32,512,1]{3,2,1,0,4:T(8,128)(2,1)S(1)} %convert_bitcast_fusion) | data formatting | bytes 4194304 | tf_op jit(solution)/shard_map/convert_element_type | solution.py:34
  166.7 0.0 copy-done.3
  166.7 0.1 copy.44
  166.8 8.9 %all_gather.19 = bf16[2,64,512]{1,0,2:T(2,128)(2,1)S(1)} all-gather(bf16[2,64,64]{1,0,2:T(2,128)(2,1)S(1)} %copy.44), channel_id=1, replica_groups=mesh['kt'=4,'ks'=8] {'ks'}, dimensions={2}, use_global_device_ids=true | all-gather | bytes 147456 | tf_op jit(solution)/shard_map/all_gather | solution.py:10
  175.8 0.0 all-to-all-done
  175.8 2.6 copy.41
  178.4 6.6 %fusion.3 = bf16[2,4,32,32,512]{4,3,2,1,0:T(8,128)(2,1)} fusion(bf16[2,4,512,512,1]{3,2,4,1,0:T(8,128)(2,1)S(1)} %bitcast.37, f32[4,32,512]{2,1,0:T(8,128)S(1)} %convert_element_type.35, f32[2,32,512]{2,1,0:T(8,128)S(1)} %convert_element_type.34), kind=kOutput, calls=%fused_computation.6 | convolution fusion | flops 4307550208 | bytes 12976128 | tf_op jit(solution)/shard_map/tsvwp,tspq->tsvwq/dot_general | solution.py:39
  185.1 44.4 %copy.43 = bf16[2,4,32,32,512]{3,2,1,0,4:T(8,128)(2,1)} copy(bf16[2,4,32,32,512]{4,3,2,1,0:T(8,128)(2,1)} %fusion.3) | data formatting | bytes 16777216 | tf_op jit(solution)/shard_map/convert_element_type | solution.py:41
  229.4 0.0 copy-start.5
  229.5 28.2 %fusion.4 = bf16[2,32,16,512]{1,2,0,3:T(8,128)(2,1)} fusion(bf16[4,16,32,512,1]{2,1,0,4,3:T(8,128)(2,1)} %copy.50, bf16[2,4,32,32,512]{3,2,1,0,4:T(8,128)(2,1)} %copy.43), kind=kOutput, calls=%fused_computation.7 | convolution fusion | flops 134742016 | bytes 11534336 | tf_op jit(solution)/shard_map/tsvwq,snwq->tvnq/dot_general | solution.py:42
  257.6 5.2 %copy.45 = bf16[2,32,16,512]{3,2,1,0:T(8,128)(2,1)S(1)} copy(bf16[2,32,16,512]{1,2,0,3:T(8,128)(2,1)} %fusion.4) | data formatting | bytes 2097152 | tf_op jit(solution)/shard_map/convert_element_type | solution.py:44
  262.9 0.4 fusion.5
  263.3 0.1 copy.47
  263.4 0.9 convert_element_type.42
  264.3 0.0 all-reduce.3.cloned.1.call-update
  264.4 0.0 copy-done.5
  264.4 0.6 dynamic-slice
  265.6 50.4 %all-reduce.3.cloned.1.call-done = bf16[2,16,2048]{2,1,0:T(8,128)(2,1)} async-done(((bf16[2,16,2048]{2,1,0:T(8,128)(2,1)}), bf16[2,16,2048]{2,1,0:T(8,128)(2,1)}) %all-reduce.3.cloned.1.call-update) | async-done | bytes 131088
  316.0 1.5 dynamic-slice_convert_fusion
  (4 shorter events, 0.0 us)
Async XLA Ops:
  13.8 12.3 %copy-start.4 = (bf16[2,32,64]{2,1,0:T(8,128)(2,1)S(1)}, bf16[2,32,64]{2,1,0:T(8,128)(2,1)}, u32[]{:S(2)}) copy-start(bf16[2,32,64]{2,1,0:T(8,128)(2,1)} %param.7) | copy-start | bytes 24580
  13.8 46.1 %copy-start.2 = (bf16[4,32,128]{2,1,0:T(8,128)(2,1)S(1)}, bf16[4,32,128]{2,1,0:T(8,128)(2,1)}, u32[]{:S(2)}) copy-start(bf16[4,32,128]{2,1,0:T(8,128)(2,1)} %param.9) | copy-start | bytes 98308
  13.8 112.8 %copy-start.1 = (bf16[4,4,2048]{2,1,0:T(4,128)(2,1)S(1)}, bf16[4,4,2048]{2,1,0:T(4,128)(2,1)}, u32[]{:S(2)}) copy-start(bf16[4,4,2048]{2,1,0:T(4,128)(2,1)} %param.11) | copy-start | bytes 196612
  13.8 127.4 %copy-start = (bf16[4,64,128]{2,1,0:T(8,128)(2,1)S(1)}, bf16[4,64,128]{2,1,0:T(8,128)(2,1)}, u32[]{:S(2)}) copy-start(bf16[4,64,128]{2,1,0:T(8,128)(2,1)} %param.10) | copy-start | bytes 196612
  18.6 157.2 %all-to-all-start = ((bf16[8,32,16,512]{3,2,0,1:T(8,128)(2,1)}), bf16[8,32,16,512]{3,2,0,1:T(8,128)(2,1)}, u32[]{:S(2)}, u32[]{:S(2)}) async-start(bf16[8,32,16,512]{3,2,0,1:T(8,128)(2,1)} %copy.40), calls=%async_computation | async-start | bytes 8388608 | tf_op jit(solution)/shard_map/all_to_all | solution.py:29
  26.1 289.9 %all-reduce.3.cloned.1.call-start = ((), (), s32[]{:S(2)}) async-start(), calls=%async_computation.1 | async-start | bytes 262144
  26.2 140.5 %copy-start.3 = (bf16[2,64,64]{2,1,0:T(8,128)(2,1)S(1)}, bf16[2,64,64]{2,1,0:T(8,128)(2,1)}, u32[]{:S(2)}) copy-start(bf16[2,64,64]{2,1,0:T(8,128)(2,1)} %param.8) | copy-start | bytes 49156
  229.4 34.9 %copy-start.5 = (u32[32]{0:T(128)S(1)}, u32[32]{0:T(128)}, u32[]{:S(2)}) copy-start(u32[32]{0:T(128)} %constant.12) | copy-start | bytes 388
Sparse Core Ops, SparseCore 0:
  264.5 51.4 all-reduce.2
where the time goes:
time: 325 us; the launch traced here: 324 us
  blocking collectives  136 us (42%)
  local copies, waits for them, and re-layouts  78.9 us (24%)
  waiting for transfers between devices  50.4 us (16%)
  matrix products  35.9 us (11%)
  between operations  14.2 us (4%)
  starting transfers between devices  7.5 us (2%)
    all_gather x1, blocking collectives, local(): lax.all_gather(val_source, 'kt', axis=2, tiled=True)  66.6 us
    unnamed x2, waiting for transfers between devices  50.4 us
    convert_element_type x1, local copies, waits for them, and re-layouts, local(): kernels = jnp.einsum('tsvwp,tspq->tsvwq', pair_prod, pair_mats, preferred...  44.4 us
    all_gather x1, blocking collectives, local(): lax.all_gather(val_target, 'ks', axis=2, tiled=True)  33.5 us
    dot_general x1, matrix products, local(): jnp.einsum('tsvwq,snwq->tvnq', kernels, dressed, preferred_element_type=j...  28.2 us
    all_gather x1, blocking collectives, local(): lax.all_gather(trial_vectors, 'kt', axis=1, tiled=True)  13.9 us
    all_gather x1, blocking collectives, local(): lax.all_gather(cond_source, 'kt', axis=2, tiled=True)  12.8 us
    convert_element_type x1, local copies, waits for them, and re-layouts, local(): dressed = jnp.einsum('snwc,scq->snwq', trial_four, src_cond, preferred_el...  12 us
  transfers between devices with their start and end apart: 2, of which 1 were waited for; matrix products, arithmetic and copies ran while one was open for 4% of the time, Pallas kernels for 0%

commit v1 on v0

--- a/solution.py
+++ b/solution.py
@@ -1,10 +1,14 @@
+import functools
+
 import jax
 import jax.numpy as jnp
 from jax import lax
+from jax.experimental import pallas as pl
+from jax.experimental.pallas import tpu as pltpu
 from jax.sharding import PartitionSpec as P
 
 
-def local(val_target, cond_target, val_source, cond_source, trial_vectors, screened, pair_momentum):
+def general(val_target, cond_target, val_source, cond_source, trial_vectors, screened, pair_momentum):
     tgt_val, tgt_cond = (
         lax.all_gather(val_target, "ks", axis=2, tiled=True),
         lax.all_gather(cond_target, "ks", axis=2, tiled=True),
@@ -51,6 +55,316 @@
     ).astype(jnp.float32)
 
 
+MESH = pl.DeviceIdType.MESH
+VMEM = pl.BlockSpec(memory_space=pltpu.VMEM)
+
+
+def remote(src, dst, send, recv, kt, ks):
+    return pltpu.make_async_remote_copy(
+        src_ref=src, dst_ref=dst, send_sem=send, recv_sem=recv, device_id=(kt, ks), device_id_type=MESH
+    )
+
+
+def greet(peers):
+    barrier = pltpu.get_barrier_semaphore()
+    for kt, ks in peers:
+        pl.semaphore_signal(barrier, inc=1, device_id=(kt, ks), device_id_type=MESH)
+    pl.semaphore_wait(barrier, len(peers))
+
+
+def gather_kernel(nz, ns, block, vsx, vtx, out, vsg, vtg,
+                  zs, zr, xs, xr, ys, yr, as_, ar, bs, br, ps, pr, vss, vsr, vts, vtr, ls):
+    z, k = lax.axis_index("kt"), lax.axis_index("ks")
+    core = lax.rem(k, 2)
+    side = lax.rem(k // 2, 2)
+    kx = k + 2 - 4 * side
+    ky = lax.rem(k + 4, ns)
+    kd = lax.rem(kx + 4, ns)
+    kp = k + 1 - 2 * core
+    half = block.shape[0] // 2
+    first, second = pl.ds(0, half), pl.ds(half, half)
+    zpeer = [lax.rem(z + j, nz) for j in range(nz)]
+    speer = [lax.rem(k + j, ns) for j in range(ns)]
+    greet([(zpeer[j], k) for j in range(1, nz)] + [(z, speer[j]) for j in range(1, ns)])
+
+    slot = lambda zz, kk: out.at[zz * ns + kk]
+    started = []
+
+    def go(copy):
+        copy.start()
+        started.append(copy)
+
+    def arrived(dst, recv):
+        remote(dst, dst, recv, recv, z, kp).wait_recv()
+
+    def partner(index, src, zz, kk):
+        go(remote(src, slot(zz, kk), ps.at[index], pr.at[index], z, kp))
+
+    for j in (1, nz - 1, *range(2, nz - 1)):
+        go(remote(block, slot(z, k), zs.at[j], zr.at[nz - j], zpeer[j], k))
+    go(remote(block, slot(z, k), xs.at[0], xr.at[0], z, kx))
+    go(remote(block, slot(z, k), ys.at[0], yr.at[0], z, ky))
+    partner(0, block, z, k)
+    for j in range(1, ns):
+        go(remote(vsx.at[speer[j]], vsg.at[k], vss.at[j], vsr.at[j], z, speer[j]))
+        go(remote(vtx, vtg.at[k], vts.at[j], vtr.at[j], z, speer[j]))
+    own = [
+        pltpu.make_async_copy(block, slot(z, k), ls.at[0]),
+        pltpu.make_async_copy(vsx.at[k], vsg.at[k], ls.at[1]),
+        pltpu.make_async_copy(vtx, vtg.at[k], ls.at[2]),
+    ]
+    for copy in own:
+        copy.start()
+
+    order = [0, 1, nz - 1, *range(2, nz - 1)]
+
+    def relay(j):
+        zz = zpeer[j]
+        arrived(slot(zz, kx), xr.at[j])
+        go(remote(slot(zz, kx).at[first], slot(zz, kx).at[first], as_.at[j], ar.at[j], z, ky))
+        partner(nz + j, slot(zz, kx), zz, kx)
+        arrived(slot(zz, ky), yr.at[j])
+        go(remote(slot(zz, ky).at[second], slot(zz, ky).at[second], bs.at[j], br.at[j], z, kx))
+        partner(2 * nz + j, slot(zz, ky), zz, ky)
+
+    def corner(j):
+        zz = zpeer[j]
+        arrived(slot(zz, kd).at[first], ar.at[j])
+        arrived(slot(zz, kd).at[second], br.at[j])
+        partner(3 * nz + j, slot(zz, kd), zz, kd)
+
+    for place, j in enumerate(order):
+        if place:
+            zz = zpeer[j]
+            arrived(slot(zz, k), zr.at[j])
+            go(remote(slot(zz, k), slot(zz, k), xs.at[j], xr.at[j], z, kx))
+            go(remote(slot(zz, k), slot(zz, k), ys.at[j], yr.at[j], z, ky))
+            partner(j, slot(zz, k), zz, k)
+            relay(order[place - 1])
+        if place > 1:
+            corner(order[place - 2])
+    relay(order[-1])
+    corner(order[-2])
+    corner(order[-1])
+
+    other = [kp, kx + 1 - 2 * core, lax.rem(kp + 4, ns), lax.rem(kx + 5 - 2 * core, ns)]
+    for j in range(nz):
+        for piece in range(4):
+            arrived(slot(zpeer[j], other[piece]), pr.at[piece * nz + j])
+    for j in range(1, ns):
+        arrived(vsg.at[speer[ns - j]], vsr.at[j])
+        arrived(vtg.at[speer[ns - j]], vtr.at[j])
+    for copy in own:
+        copy.wait()
+    for copy in started:
+        copy.wait_send()
+
+
+def contract_kernel(nz, ns, nt, nsl, table, screened, gathered, vsg, out, wbuf, wide, mbuf, abuf, sem):
+    pairs, rows, width = wbuf.shape
+    src = ns * nsl
+    tgt = nz * nt
+    nvec = mbuf.shape[1] // rows
+    lanes = 128
+    halves = nvec // nz // 2
+
+    def fetch(i, carry):
+        pltpu.make_async_copy(screened.at[table[i]], wbuf.at[i], sem).start()
+        return carry
+
+    lax.fori_loop(0, pairs, fetch, 0)
+
+    depth = vsg.shape[2] // nsl
+    shape = (nsl * rows, nsl * depth)
+    picked = lax.broadcasted_iota(jnp.int32, shape, 0) // rows == lax.broadcasted_iota(jnp.int32, shape, 1) // depth
+    low = lax.broadcasted_iota(jnp.int32, (rows, lanes), 1) < lanes // 2
+    trial_rows = halves * nsl * depth
+    cond = lanes // 2
+
+    def build(b, carry):
+        left = jnp.concatenate([vsg[b].astype(jnp.float32)] * nsl, axis=0)
+        left = jnp.where(picked, left, 0.0).astype(jnp.bfloat16)
+        right = jnp.concatenate(
+            [gathered[z * ns + b, h * nsl * depth:(h + 1) * nsl * depth, :] for z in range(nz) for h in range(halves)],
+            axis=1,
+        )
+        folded = jnp.dot(left, right, preferred_element_type=jnp.float32)
+        for s in range(nsl):
+            parts = []
+            for j in range(nvec // 2):
+                piece = folded[s * rows:(s + 1) * rows, j * lanes:(j + 1) * lanes]
+                parts += [jnp.where(low, piece, 0.0), jnp.where(low, 0.0, piece)]
+            left_s = jnp.concatenate(parts, axis=0).astype(jnp.bfloat16)
+            at = trial_rows + s * cond
+            cond_s = jnp.concatenate([gathered[z * ns + b, at:at + cond, :] for z in range(nz)], axis=1)
+            right_s = jnp.concatenate([cond_s, cond_s], axis=0)
+            mbuf[b * nsl + s] = jnp.dot(left_s, right_s, preferred_element_type=jnp.float32)
+        return carry
+
+    lax.fori_loop(0, ns, build, 0)
+    pltpu.make_async_copy(wbuf, wbuf, sem).wait()
+
+    def widen(i, carry):
+        wide[i] = wbuf[i].astype(jnp.float32)
+        return carry
+
+    lax.fori_loop(0, pairs, widen, 0, unroll=4)
+
+    group = 4
+    rblocks, qblocks = rows // 8, width // lanes
+
+    def tile(i, carry):
+        q = pl.ds(pl.multiple_of(lax.rem(i, qblocks) * lanes, lanes), lanes)
+        rest = i // qblocks
+        r = lax.rem(rest, rblocks) * 8
+        n0 = (rest // rblocks) * group
+        wrow = pl.ds(pl.multiple_of(r, 8), 8)
+        mrow = [pl.ds(pl.multiple_of((n0 + g) * rows + r, 8), 8) for g in range(group)]
+
+        def step(s, total):
+            m = [mbuf[s, mrow[g], q] for g in range(group)]
+            new = []
+            for t in range(tgt):
+                w = wide[t * src + s, wrow, q]
+                new += [total[t * group + g] + w * m[g] for g in range(group)]
+            return tuple(new)
+
+        total = lax.fori_loop(0, src, step, tuple(jnp.zeros((8, lanes), jnp.float32) for _ in range(tgt * group)), unroll=2)
+        for t in range(tgt):
+            for g in range(group):
+                abuf[t, mrow[g], q] = total[t * group + g]
+        return carry
+
+    lax.fori_loop(0, (nvec // group) * rblocks * qblocks, tile, 0)
+
+    lowc = lax.broadcasted_iota(jnp.int32, (nvec * rows, lanes), 1) < lanes // 2
+    at = trial_rows + nsl * cond
+    for z in range(nz):
+        right = jnp.concatenate([gathered[z * ns + b, at:, :] for b in range(ns)], axis=0)
+        pair = [jnp.dot(abuf[z * nt + t].astype(jnp.bfloat16), right, preferred_element_type=jnp.float32) for t in range(nt)]
+        out[z] = jnp.where(lowc, pair[0], pair[1]).astype(jnp.bfloat16)
+
+
+def finish_kernel(nz, ns, sent, vtg, out, got, ss, rs, ls):
+    z, k = lax.axis_index("kt"), lax.axis_index("ks")
+    me = z * ns + k
+    count = nz * ns
+    barrier = pltpu.get_barrier_semaphore()
+
+    def hello(j, carry):
+        peer = lax.rem(me + j, count)
+        pl.semaphore_signal(barrier, inc=1, device_id=(peer // ns, lax.rem(peer, ns)), device_id_type=MESH)
+        return carry
+
+    lax.fori_loop(1, count, hello, 0)
+    pl.semaphore_wait(barrier, count - 1)
+
+    def copy(j):
+        peer = lax.rem(me + j, count)
+        return remote(sent.at[peer], got.at[me], ss.at[j], rs.at[j], peer // ns, lax.rem(peer, ns))
+
+    def go(j, carry):
+        copy(j).start()
+        return carry
+
+    lax.fori_loop(1, count, go, 0)
+    own = pltpu.make_async_copy(sent.at[me], got.at[me], ls)
+    own.start()
+    own.wait()
+
+    def finish(j, carry):
+        copy(j).wait_send()
+        giver = got.at[lax.rem(me + count - j, count)]
+        remote(giver, giver, ss.at[j], rs.at[j], z, k).wait_recv()
+        return carry
+
+    lax.fori_loop(1, count, finish, 0)
+    nloc, both, bands = out.shape[0], out.shape[1], out.shape[2]
+    rows = got.shape[1] // nloc
+    left = jnp.concatenate([vtg[b] for b in range(ns)], axis=1)
+    for n in range(nloc):
+        right = jnp.concatenate([got[i, n * rows:(n + 1) * rows, :] for i in range(count)], axis=0)
+        out[n] = jnp.dot(left, right, preferred_element_type=jnp.float32)
+
+
+def local(val_target, cond_target, val_source, cond_source, trial_vectors, screened, pair_momentum):
+    nz, ns = lax.axis_size("kt"), lax.axis_size("ks")
+    nt, bands, pk = val_target.shape
+    nc = cond_target.shape[1]
+    nsl, _, pz = val_source.shape
+    nv = trial_vectors.shape[1]
+    rows, width = screened.shape[1:]
+    nvec = nv * nz
+    bf16, f32 = jnp.bfloat16, jnp.float32
+    trial = trial_vectors.reshape(nsl, nv // 2, 2, bands, nc).transpose(1, 0, 3, 2, 4).reshape(-1, 2 * nc)
+    block = jnp.concatenate(
+        [trial, cond_source.reshape(nsl * nc, pz), cond_target.transpose(2, 0, 1).reshape(pk, nt * nc)], axis=0
+    )
+    vsx = val_source.reshape(nsl, bands, ns, rows).transpose(2, 3, 0, 1).reshape(ns, rows, nsl * bands)
+    vtx = val_target.reshape(nt * bands, pk)
+    dma = pltpu.SemaphoreType.DMA
+    gathered, vsg, vtg = pl.pallas_call(
+        functools.partial(gather_kernel, nz, ns),
+        out_shape=(
+            jax.ShapeDtypeStruct((nz * ns, *block.shape), bf16),
+            jax.ShapeDtypeStruct(vsx.shape, bf16),
+            jax.ShapeDtypeStruct((ns, *vtx.shape), bf16),
+        ),
+        in_specs=[VMEM] * 3,
+        out_specs=(VMEM,) * 3,
+        scratch_shapes=[dma((nz,))] * 10 + [dma((4 * nz,))] * 2 + [dma((ns,))] * 4 + [dma((3,))],
+        compiler_params=pltpu.CompilerParams(collective_id=0, has_side_effects=True),
+        name="gather",
+    )(block, vsx, vtx)
+    pairs = pair_momentum.size
+    held = pl.pallas_call(
+        functools.partial(contract_kernel, nz, ns, nt, nsl),
+        out_shape=jax.ShapeDtypeStruct((nz, nvec * rows, nt * nc), bf16),
+        in_specs=[
+            pl.BlockSpec(memory_space=pltpu.SMEM),
+            pl.BlockSpec(memory_space=pl.ANY),
+            VMEM,
+            VMEM,
+        ],
+        out_specs=VMEM,
+        scratch_shapes=[
+            pltpu.VMEM((pairs, rows, width), bf16),
+            pltpu.VMEM((pairs, rows, width), f32),
+            pltpu.VMEM((ns * nsl, nvec * rows, width), f32),
+            pltpu.VMEM((nz * nt, nvec * rows, width), f32),
+            dma,
+        ],
+        compiler_params=pltpu.CompilerParams(vmem_limit_bytes=56 * 2**20),
+        name="contract",
+    )(pair_momentum.reshape(-1), screened, gathered, vsg)
+    nloc = nvec // ns
+    sent = held.reshape(nz * ns, nloc * rows, nt * nc)
+    wide = pl.pallas_call(
+        functools.partial(finish_kernel, nz, ns),
+        out_shape=jax.ShapeDtypeStruct((nloc, nt * bands, nt * nc), f32),
+        in_specs=[VMEM] * 2,
+        out_specs=VMEM,
+        scratch_shapes=[pltpu.VMEM(sent.shape, bf16), dma((nz * ns,)), dma((nz * ns,)), dma],
+        compiler_params=pltpu.CompilerParams(collective_id=1, has_side_effects=True),
+        name="finish",
+    )(sent, vtg)
+    wide = wide.reshape(nloc, nt, bands, nt, nc)
+    result = jnp.stack([wide[:, t, :, t, :] for t in range(nt)], axis=0)
+    return result.reshape(nt, nloc, bands * nc)
+
+
+def fits(mesh, args):
+    val_target, cond_target, val_source, cond_source, trial_vectors, screened, pair_momentum = args
+    nz, ns = mesh.shape["kt"], mesh.shape["ks"]
+    aux = val_target.shape[2]
+    nt, nvec, nc = val_target.shape[0] // nz, trial_vectors.shape[1], cond_target.shape[1]
+    rows = aux // (nz * ns)
+    return (
+        ns == 8 and nz >= 3 and nt == 2 and 2 * nc == 128 and aux // nz == 128 and rows == 16
+        and nvec % (2 * nz) == 0 and nvec % ns == 0 and pair_momentum.size <= 256
+    )
+
+
 def solution(mesh):
     in_specs = (
         P("kt", None, "ks"),
@@ -62,4 +376,9 @@
         P(),
     )
     out_specs = P("kt", "ks", None)
-    return jax.shard_map(local, mesh=mesh, in_specs=in_specs, out_specs=out_specs, check_vma=False)
+
+    def whole(*args):
+        body = local if fits(mesh, args) else general
+        return jax.shard_map(body, mesh=mesh, in_specs=in_specs, out_specs=out_specs, check_vma=False)(*args)
+
+    return whole

time: 325 us -> 87.3 us (0.27)
  blocking collectives: 136 us -> 0 us
  Pallas kernels: 0 us -> 78.2 us
  local copies, waits for them, and re-layouts: 78.9 us -> 6.46 us
  waiting for transfers between devices: 50.4 us -> 0 us
  matrix products: 35.9 us -> 0 us
  between operations: 14.2 us -> 0.08 us
  starting transfers between devices: 7.5 us -> 0 us
    all_gather x5 -> x0, blocking collectives: 136 us -> none  [the longest x1 66.6 us: local(): lax.all_gather(val_source, 'kt', axis=2, tiled=True)]
    pallas_call x0 -> x3, Pallas kernels: none -> 78.2 us  [the longest x1 37.3 us: local(): pl.pallas_call(functools.partial(gather_kernel, nz, ns), out_shape=(jax.S...]
    convert_element_type x5 -> x0, local copies, waits for them, and re-layouts: 62.6 us -> none  [the longest x1 44.4 us: local(): kernels = jnp.einsum('tsvwp,tspq->tsvwq', pair_prod, pair_mats, preferred...]
    unnamed x2 -> x0, waiting for transfers between devices: 50.4 us -> none
    dot_general x4 -> x0, matrix products: 35.9 us -> none  [the longest x1 28.2 us: local(): jnp.einsum('tsvwq,snwq->tvnq', kernels, dressed, preferred_element_type=j...]
    gather x2 -> x0, local copies, waits for them, and re-layouts: 11 us -> none  [local(): outgoing = screened[table]]
    all_to_all x1 -> x0, starting transfers between devices: 7.45 us -> none  [local(): lax.all_to_all(outgoing, ('kt', 'ks'), split_axis=1, concat_axis=1, tiled...]
    reshape x3 -> x7, local copies, waits for them, and re-layouts: 1.35 us -> 5.11 us  [the longest x1 1.35 us: local(): pair_momentum.reshape(-1)]
  transfers between devices with their start and end apart: 2 -> 0, of which waited for: 1 -> 0; matrix products, arithmetic and copies ran while one was open for 4% -> 0% of each run, Pallas kernels for 0% -> 0%
where the time goes in v1:
time: 87.3 us; the launch traced here: 86.9 us
  Pallas kernels  78.2 us (90%)
  local copies, waits for them, and re-layouts  6.46 us (7%)
  other arithmetic  2.15 us (2%)
    pallas_call x1, Pallas kernels, local(): pl.pallas_call(functools.partial(gather_kernel, nz, ns), out_shape=(jax.S...  37.3 us
    pallas_call x1, Pallas kernels, local(): pl.pallas_call(functools.partial(contract_kernel, nz, ns, nt, nsl), out_s...  28.7 us
    pallas_call x1, Pallas kernels, local(): pl.pallas_call(functools.partial(finish_kernel, nz, ns), out_shape=jax.Sh...  12.2 us

profile of v1, /device:TPU:0, one launch (start us, length us, event | category | flops | bytes accessed | tf_op | source)
XLA Modules:
  0.0 86.9 jit_solution(13278680954328943435)
XLA Ops:
  0.0 1.4 %reshape.35.table = s32[256]{0:T(256)} reshape(s32[8,32]{1,0:T(8,128)} %param.13) | data formatting | bytes 2048 | tf_op jit(solution)/shard_map/reshape | solution.py:339
  1.4 0.8 copy.15
  2.2 0.9 %copy.13 = bf16[4,32,128]{1,2,0:T(8,128)(2,1)S(1)} copy(bf16[4,32,128]{2,1,0:T(8,128)(2,1)} %param.9) | data formatting | bytes 65536 | tf_op args[2]
  3.1 0.1 copy.14
  3.2 0.7 reshape.41.vsx
  3.9 1.0 %reshape.36 = bf16[4,2,2,32,64]{4,3,2,1,0:T(8,128)(2,1)S(1)} reshape(bf16[4,4,2048]{2,1,0:T(4,128)(2,1)} %param.11) | data formatting | bytes 131072 | tf_op jit(solution)/shard_map/reshape | solution.py:299
  4.9 0.1 copy.17
  5.1 0.1 reshape.37
  5.2 1.5 %pad_maximum_fusion.block = bf16[576,128]{1,0:T(8,128)(2,1)} fusion(bf16[64,128]{1,0:T(8,128)(2,1)S(1)} %copy.15, bf16[256,128]{1,0:T(8,128)(2,1)} %bitcast.15, bf16[256,128]{1,0:T(8,128)(2,1)S(1)} %reshape.37), kind=kLoop, calls=%fused_computation | loop fusion | flops 442368 | bytes 294912 | tf_op jit(solution)/shard_map/concatenate | solution.py:300
  6.7 37.3 %gather.1 = (bf16[32,576,128]{2,1,0:T(8,128)(2,1)}, bf16[8,16,128]{2,1,0:T(8,128)(2,1)}, bf16[8,64,64]{2,1,0:T(8,128)(2,1)}) custom-call(bf16[576,128]{1,0:T(8,128)(2,1)} %pad_maximum_fusion.block, bf16[8,16,128]{2,1,0:T(8,128)(2,1)} %reshape.41.vsx, bf16[64,64]{1,0:T(8,128)(2,1)} %bitcast.17), custom_call_target="tpu_custom_call" | custom-call | tf_op jit(solution)/shard_map/gather/pallas_call | solution.py:306
  44.0 28.7 %contract.1 = bf16[4,256,128]{2,1,0:T(8,128)(2,1)} custom-call(s32[256]{0:T(256)} %reshape.35.table, bf16[512,16,512]{2,1,0:T(8,128)(2,1)} %screened.1, bf16[32,576,128]{2,1,0:T(8,128)(2,1)} %get-tuple-element.8.gathered, bf16[8,16,128]{2,1,0:T(8,128)(2,1)} %get-tuple-element.9.vsg), custom_call_target="tpu_custom_call" | custom-call | tf_op jit(solution)/shard_map/contract/pallas_call | solution.py:320
  72.7 12.2 %finish.1 = f32[2,64,128]{2,1,0:T(8,128)} custom-call(bf16[32,32,128]{2,1,0:T(8,128)(2,1)} %bitcast.12, bf16[8,64,64]{2,1,0:T(8,128)(2,1)} %get-tuple-element.10.vtg), custom_call_target="tpu_custom_call" | custom-call | tf_op jit(solution)/shard_map/finish/pallas_call | solution.py:342
  84.9 1.0 %reshape.44 = f32[2,2,32,2,64]{4,3,2,1,0:T(2,128)S(1)} reshape(f32[2,64,128]{2,1,0:T(8,128)} %finish.1) | data formatting | bytes 131072 | tf_op jit(solution)/shard_map/reshape | solution.py:351
  85.9 0.2 slice_reduce_fusion.1
  86.1 0.1 stack.7
  86.2 0.1 stack.8
  86.2 0.6 pad_maximum_fusion.1

commit v2 on v0

--- a/solution.py
+++ b/solution.py
@@ -1,10 +1,14 @@
+import functools
+
 import jax
 import jax.numpy as jnp
 from jax import lax
+from jax.experimental import pallas as pl
+from jax.experimental.pallas import tpu as pltpu
 from jax.sharding import PartitionSpec as P
 
 
-def local(val_target, cond_target, val_source, cond_source, trial_vectors, screened, pair_momentum):
+def general(val_target, cond_target, val_source, cond_source, trial_vectors, screened, pair_momentum):
     tgt_val, tgt_cond = (
         lax.all_gather(val_target, "ks", axis=2, tiled=True),
         lax.all_gather(cond_target, "ks", axis=2, tiled=True),
@@ -51,6 +55,306 @@
     ).astype(jnp.float32)
 
 
+MESH = pl.DeviceIdType.MESH
+VMEM = pl.BlockSpec(memory_space=pltpu.VMEM)
+
+
+def remote(src, dst, send, recv, kt, ks):
+    return pltpu.make_async_remote_copy(
+        src_ref=src, dst_ref=dst, send_sem=send, recv_sem=recv, device_id=(kt, ks), device_id_type=MESH
+    )
+
+
+def fused_kernel(nz, ns, nt, nsl, table, screened, block, vsx, vtx, result,
+                 out, vsg, vtg, slab, wide, mbuf, abuf, sent, got,
+                 zs, zr, xs, xr, ys, yr, as_, ar, bs, br, ps, pr, vss, vsr, vts, vtr, fs, fr, ls):
+    z, k = lax.axis_index("kt"), lax.axis_index("ks")
+    core = lax.rem(k, 2)
+    side = lax.rem(k // 2, 2)
+    kx = k + 2 - 4 * side
+    ky = lax.rem(k + 4, ns)
+    kd = lax.rem(kx + 4, ns)
+    kp = k + 1 - 2 * core
+    other = [kp, kx + 1 - 2 * core, lax.rem(kp + 4, ns), lax.rem(kx + 5 - 2 * core, ns)]
+    half = block.shape[0] // 2
+    first, second = pl.ds(0, half), pl.ds(half, half)
+    zpeer = [lax.rem(z + j, nz) for j in range(nz)]
+    speer = [lax.rem(k + j, ns) for j in range(ns)]
+    me = z * ns + k
+    count = nz * ns
+
+    load = pltpu.make_async_copy(screened, slab, ls.at[3])
+    load.start()
+    own = [
+        pltpu.make_async_copy(block, out.at[me], ls.at[0]),
+        pltpu.make_async_copy(vsx.at[k], vsg.at[k], ls.at[1]),
+        pltpu.make_async_copy(vtx, vtg.at[k], ls.at[2]),
+    ]
+    for copy in own:
+        copy.start()
+
+    barrier = pltpu.get_barrier_semaphore()
+
+    def hello(j, carry):
+        peer = lax.rem(me + j, count)
+        pl.semaphore_signal(barrier, inc=1, device_id=(peer // ns, lax.rem(peer, ns)), device_id_type=MESH)
+        return carry
+
+    lax.fori_loop(1, count, hello, 0)
+    pl.semaphore_wait(barrier, count - 1)
+
+    slot = lambda zz, kk: out.at[zz * ns + kk]
+    started = []
+
+    def go(copy):
+        copy.start()
+        started.append(copy)
+
+    def arrived(dst, recv):
+        remote(dst, dst, recv, recv, z, kp).wait_recv()
+
+    def partner(index, src, zz, kk):
+        go(remote(src, slot(zz, kk), ps.at[index], pr.at[index], z, kp))
+
+    for j in range(1, ns):
+        go(remote(vsx.at[speer[j]], vsg.at[k], vss.at[j], vsr.at[j], z, speer[j]))
+    for j in (1, nz - 1, *range(2, nz - 1)):
+        go(remote(block, slot(z, k), zs.at[j], zr.at[nz - j], zpeer[j], k))
+    go(remote(block, slot(z, k), xs.at[0], xr.at[0], z, kx))
+    go(remote(block, slot(z, k), ys.at[0], yr.at[0], z, ky))
+    partner(0, block, z, k)
+    for j in range(1, ns):
+        go(remote(vtx, vtg.at[k], vts.at[j], vtr.at[j], z, speer[j]))
+
+    order = [0, 1, nz - 1, *range(2, nz - 1)]
+
+    def spread(j):
+        zz = zpeer[j]
+        arrived(slot(zz, k), zr.at[j])
+        go(remote(slot(zz, k), slot(zz, k), xs.at[j], xr.at[j], z, kx))
+        go(remote(slot(zz, k), slot(zz, k), ys.at[j], yr.at[j], z, ky))
+        partner(j, slot(zz, k), zz, k)
+
+    def relay(j):
+        zz = zpeer[j]
+        arrived(slot(zz, kx), xr.at[j])
+        go(remote(slot(zz, kx).at[first], slot(zz, kx).at[first], as_.at[j], ar.at[j], z, ky))
+        partner(nz + j, slot(zz, kx), zz, kx)
+        arrived(slot(zz, ky), yr.at[j])
+        go(remote(slot(zz, ky).at[second], slot(zz, ky).at[second], bs.at[j], br.at[j], z, kx))
+        partner(2 * nz + j, slot(zz, ky), zz, ky)
+
+    def corner(j):
+        zz = zpeer[j]
+        arrived(slot(zz, kd).at[first], ar.at[j])
+        arrived(slot(zz, kd).at[second], br.at[j])
+        partner(3 * nz + j, slot(zz, kd), zz, kd)
+
+    def passed(piece):
+        for j in range(nz):
+            arrived(slot(zpeer[j], other[piece]), pr.at[piece * nz + j])
+
+    rows, width = slab.shape[1:]
+    tgt = nz * nt
+    nvec = mbuf.shape[1] // rows
+    lanes = 128
+    halves = nvec // nz // 2
+    depth = vsg.shape[2] // nsl
+    shape = (nsl * rows, nsl * depth)
+    picked = lax.broadcasted_iota(jnp.int32, shape, 0) // rows == lax.broadcasted_iota(jnp.int32, shape, 1) // depth
+    trial_rows = halves * nsl * depth
+    cond = lanes // 2
+    group = 4
+    rblocks, qblocks = rows // 8, width // lanes
+
+    def compute(b, fresh=False):
+        low = lax.broadcasted_iota(jnp.int32, (rows, lanes), 1) < lanes // 2
+        left = jnp.concatenate([vsg[b].astype(jnp.float32)] * nsl, axis=0)
+        left = jnp.where(picked, left, 0.0).astype(jnp.bfloat16)
+        right = jnp.concatenate(
+            [out[zz * ns + b, h * nsl * depth:(h + 1) * nsl * depth, :] for zz in range(nz) for h in range(halves)],
+            axis=1,
+        )
+        folded = jnp.dot(left, right, preferred_element_type=jnp.float32)
+        for s in range(nsl):
+            parts = []
+            for j in range(nvec // 2):
+                piece = folded[s * rows:(s + 1) * rows, j * lanes:(j + 1) * lanes]
+                parts += [jnp.where(low, piece, 0.0), jnp.where(low, 0.0, piece)]
+            left_s = jnp.concatenate(parts, axis=0).astype(jnp.bfloat16)
+            at = trial_rows + s * cond
+            cond_s = jnp.concatenate([out[zz * ns + b, at:at + cond, :] for zz in range(nz)], axis=1)
+            right_s = jnp.concatenate([cond_s, cond_s], axis=0)
+            mbuf[s] = jnp.dot(left_s, right_s, preferred_element_type=jnp.float32)
+
+        def widen(t, carry):
+            for s in range(nsl):
+                wide[t * nsl + s] = slab[table[t, b * nsl + s]].astype(jnp.float32)
+            return carry
+
+        lax.fori_loop(0, tgt, widen, 0)
+
+        def tile(i, carry):
+            q = pl.ds(pl.multiple_of(lax.rem(i, qblocks) * lanes, lanes), lanes)
+            rest = i // qblocks
+            r = lax.rem(rest, rblocks) * 8
+            n0 = (rest // rblocks) * group
+            wrow = pl.ds(pl.multiple_of(r, 8), 8)
+            mrow = [pl.ds(pl.multiple_of((n0 + g) * rows + r, 8), 8) for g in range(group)]
+            total = {}
+            for s in range(nsl):
+                m = [mbuf[s, mrow[g], q] for g in range(group)]
+                for t in range(tgt):
+                    w = wide[t * nsl + s, wrow, q]
+                    for g in range(group):
+                        term = w * m[g]
+                        total[t, g] = term if s == 0 else total[t, g] + term
+            for t in range(tgt):
+                for g in range(group):
+                    value = total[t, g] if fresh else abuf[t, mrow[g], q] + total[t, g]
+                    abuf[t, mrow[g], q] = value
+            return carry
+
+        lax.fori_loop(0, (nvec // group) * rblocks * qblocks, tile, 0)
+
+    spread(order[1])
+    relay(order[0])
+    spread(order[2])
+    relay(order[1])
+    corner(order[0])
+    for j in order[3:]:
+        spread(j)
+    for copy in own:
+        copy.wait()
+    for j in range(1, ns):
+        arrived(vsg.at[speer[ns - j]], vsr.at[j])
+    load.wait()
+    compute(k, True)
+    for place in range(2, nz):
+        relay(order[place])
+        corner(order[place - 1])
+        if place == 2:
+            passed(0)
+            compute(kp)
+    compute(kx)
+    corner(order[-1])
+    passed(1)
+    passed(2)
+
+    def later(i, carry):
+        one = i // 2
+        sx = lax.rem(i + 1, 2) * one + (1 - one) * lax.rem(i, 2)
+        sy = (1 - one) + one * lax.rem(i, 2)
+        kc = k + one * (1 - 2 * core)
+        compute(lax.rem(kc + sx * (2 - 4 * side) + 4 * sy, ns))
+        return carry
+
+    lax.fori_loop(0, 4, later, 0)
+    passed(3)
+    compute(other[3])
+
+    lowc = lax.broadcasted_iota(jnp.int32, (nvec * rows, lanes), 1) < lanes // 2
+    at = trial_rows + nsl * cond
+    chunk = sent.shape[1] // ns
+
+    def deal(dz, dk):
+        zz, kk = lax.rem(z + dz, nz), lax.rem(k + dk, ns)
+        src = sent.at[zz, pl.ds(pl.multiple_of(kk * chunk, chunk), chunk)]
+        return remote(src, got.at[me], fs.at[dz, dk], fr.at[dz, dk], zz, kk)
+
+    def emit(i, carry):
+        dz = lax.rem(i + 1, nz)
+        zz = lax.rem(z + dz, nz)
+        right = jnp.concatenate([out[zz * ns + b, at:, :] for b in range(ns)], axis=0)
+        pair = [jnp.dot(abuf[zz * nt + t].astype(jnp.bfloat16), right, preferred_element_type=jnp.float32) for t in range(nt)]
+        sent[zz] = jnp.where(lowc, pair[0], pair[1]).astype(jnp.bfloat16)
+
+        def push(dk, carry):
+            deal(dz, dk).start()
+            return carry
+
+        lax.fori_loop((i + 1) // nz, ns, push, 0)
+        return carry
+
+    lax.fori_loop(0, nz, emit, 0)
+    mine = pltpu.make_async_copy(sent.at[z, pl.ds(pl.multiple_of(k * chunk, chunk), chunk)], got.at[me], ls.at[4])
+    mine.start()
+    mine.wait()
+    for copy in started:
+        copy.wait_send()
+    for j in range(1, ns):
+        arrived(vtg.at[speer[ns - j]], vtr.at[j])
+
+    def settle(i, carry):
+        dz, dk = i // ns, lax.rem(i, ns)
+        deal(dz, dk).wait_send()
+        giver = got.at[lax.rem(z + nz - dz, nz) * ns + lax.rem(k + ns - dk, ns)]
+        remote(giver, giver, fs.at[dz, dk], fr.at[dz, dk], z, kp).wait_recv()
+        return carry
+
+    lax.fori_loop(1, count, settle, 0)
+    left = jnp.concatenate([vtg[b] for b in range(ns)], axis=1)
+    for n in range(result.shape[0]):
+        right = jnp.concatenate([got[i, n * rows:(n + 1) * rows, :] for i in range(count)], axis=0)
+        result[n] = jnp.dot(left, right, preferred_element_type=jnp.float32)
+
+
+def local(val_target, cond_target, val_source, cond_source, trial_vectors, screened, pair_momentum):
+    nz, ns = lax.axis_size("kt"), lax.axis_size("ks")
+    nt, bands, pk = val_target.shape
+    nc = cond_target.shape[1]
+    nsl, _, pz = val_source.shape
+    nv = trial_vectors.shape[1]
+    rows, width = screened.shape[1:]
+    nvec = nv * nz
+    nloc = nvec // ns
+    bf16, f32 = jnp.bfloat16, jnp.float32
+    trial = trial_vectors.reshape(nsl, nv // 2, 2, bands, nc).transpose(1, 0, 3, 2, 4).reshape(-1, 2 * nc)
+    block = jnp.concatenate(
+        [trial, cond_source.reshape(nsl * nc, pz), cond_target.transpose(2, 0, 1).reshape(pk, nt * nc)], axis=0
+    )
+    vsx = val_source.reshape(nsl, bands, ns, rows).transpose(2, 3, 0, 1).reshape(ns, rows, nsl * bands)
+    vtx = val_target.reshape(nt * bands, pk)
+    dma = pltpu.SemaphoreType.DMA
+    wide = pl.pallas_call(
+        functools.partial(fused_kernel, nz, ns, nt, nsl),
+        out_shape=jax.ShapeDtypeStruct((nloc, nt * bands, nt * nc), f32),
+        in_specs=[pl.BlockSpec(memory_space=pltpu.SMEM), pl.BlockSpec(memory_space=pl.ANY)] + [VMEM] * 3,
+        out_specs=VMEM,
+        scratch_shapes=[
+            pltpu.VMEM((nz * ns, *block.shape), bf16),
+            pltpu.VMEM(vsx.shape, bf16),
+            pltpu.VMEM((ns, *vtx.shape), bf16),
+            pltpu.VMEM(screened.shape, bf16),
+            pltpu.VMEM((nz * nt * nsl, rows, width), f32),
+            pltpu.VMEM((nsl, nvec * rows, width), f32),
+            pltpu.VMEM((nz * nt, nvec * rows, width), f32),
+            pltpu.VMEM((nz, nvec * rows, nt * nc), bf16),
+            pltpu.VMEM((nz * ns, nloc * rows, nt * nc), bf16),
+        ]
+        + [dma((nz,))] * 10 + [dma((4 * nz,))] * 2 + [dma((ns,))] * 4 + [dma((nz, ns))] * 2 + [dma((5,))],
+        compiler_params=pltpu.CompilerParams(
+            collective_id=0, has_side_effects=True, vmem_limit_bytes=48 * 2**20
+        ),
+        name="fused",
+    )(pair_momentum, screened, block, vsx, vtx)
+    wide = wide.reshape(nloc, nt, bands, nt, nc)
+    result = jnp.stack([wide[:, t, :, t, :] for t in range(nt)], axis=0)
+    return result.reshape(nt, nloc, bands * nc)
+
+
+def fits(mesh, args):
+    val_target, cond_target, val_source, cond_source, trial_vectors, screened, pair_momentum = args
+    nz, ns = mesh.shape["kt"], mesh.shape["ks"]
+    aux = val_target.shape[2]
+    nt, nvec, nc = val_target.shape[0] // nz, trial_vectors.shape[1], cond_target.shape[1]
+    rows = aux // (nz * ns)
+    return (
+        ns == 8 and nz >= 3 and nt == 2 and 2 * nc == 128 and aux // nz == 128 and rows == 16
+        and nvec % (2 * nz) == 0 and nvec % ns == 0 and pair_momentum.size <= 256
+    )
+
+
 def solution(mesh):
     in_specs = (
         P("kt", None, "ks"),
@@ -62,4 +366,9 @@
         P(),
     )
     out_specs = P("kt", "ks", None)
-    return jax.shard_map(local, mesh=mesh, in_specs=in_specs, out_specs=out_specs, check_vma=False)
+
+    def whole(*args):
+        body = local if fits(mesh, args) else general
+        return jax.shard_map(body, mesh=mesh, in_specs=in_specs, out_specs=out_specs, check_vma=False)(*args)
+
+    return whole

time: 325 us -> 72.8 us (0.22)
  blocking collectives: 136 us -> 0 us
  local copies, waits for them, and re-layouts: 78.9 us -> 5.05 us
  Pallas kernels: 0 us -> 65.7 us
  waiting for transfers between devices: 50.4 us -> 0 us
  matrix products: 35.9 us -> 0 us
  between operations: 14.2 us -> 0.08 us
  starting transfers between devices: 7.5 us -> 0 us
    all_gather x5 -> x0, blocking collectives: 136 us -> none  [the longest x1 66.6 us: local(): lax.all_gather(val_source, 'kt', axis=2, tiled=True)]
    pallas_call x0 -> x1, Pallas kernels: none -> 65.7 us  [local(): pl.pallas_call(functools.partial(fused_kernel, nz, ns, nt, nsl), out_shap...]
    convert_element_type x5 -> x0, local copies, waits for them, and re-layouts: 62.6 us -> none  [the longest x1 44.4 us: local(): kernels = jnp.einsum('tsvwp,tspq->tsvwq', pair_prod, pair_mats, preferred...]
    unnamed x2 -> x0, waiting for transfers between devices: 50.4 us -> none
    dot_general x4 -> x0, matrix products: 35.9 us -> none  [the longest x1 28.2 us: local(): jnp.einsum('tsvwq,snwq->tvnq', kernels, dressed, preferred_element_type=j...]
    gather x2 -> x0, local copies, waits for them, and re-layouts: 11 us -> none  [local(): outgoing = screened[table]]
    all_to_all x1 -> x0, starting transfers between devices: 7.45 us -> none  [local(): lax.all_to_all(outgoing, ('kt', 'ks'), split_axis=1, concat_axis=1, tiled...]
  transfers between devices with their start and end apart: 2 -> 0, of which waited for: 1 -> 0; matrix products, arithmetic and copies ran while one was open for 4% -> 0% of each run, Pallas kernels for 0% -> 0%
where the time goes in v2:
time: 72.8 us; the launch traced here: 72.4 us
  Pallas kernels  65.7 us (90%)
  local copies, waits for them, and re-layouts  5.05 us (7%)
  other arithmetic  1.48 us (2%)
    pallas_call x1, Pallas kernels, local(): pl.pallas_call(functools.partial(fused_kernel, nz, ns, nt, nsl), out_shap...  65.7 us
    unnamed x5, local copies, waits for them, and re-layouts  2.29 us

profile of v2, /device:TPU:0, one launch (start us, length us, event | category | flops | bytes accessed | tf_op | source)
XLA Modules:
  0.0 72.4 jit_solution(14501723586200834410)
XLA Ops:
  0.0 0.8 %copy.15 = bf16[64,128]{1,0:T(8,128)(2,1)S(1)} copy(bf16[64,128]{0,1:T(8,128)(2,1)} %bitcast.15) | data formatting | bytes 32768 | tf_op jit(solution)/shard_map/reshape | solution.py:314
  0.8 0.9 %copy.13 = bf16[4,32,128]{1,2,0:T(8,128)(2,1)S(1)} copy(bf16[4,32,128]{2,1,0:T(8,128)(2,1)} %param.9) | data formatting | bytes 65536 | tf_op args[2]
  1.7 0.1 copy.14
  1.8 0.1 reshape.34.vsx
  2.0 1.0 %reshape.29 = bf16[4,2,2,32,64]{4,3,2,1,0:T(8,128)(2,1)S(1)} reshape(bf16[4,4,2048]{2,1,0:T(4,128)(2,1)} %param.11) | data formatting | bytes 131072 | tf_op jit(solution)/shard_map/reshape | solution.py:312
  3.0 0.1 copy.17
  3.1 0.1 reshape.30
  3.2 0.9 %pad_maximum_fusion.block = bf16[576,128]{1,0:T(8,128)(2,1)S(1)} fusion(bf16[64,128]{1,0:T(8,128)(2,1)S(1)} %copy.15, bf16[256,128]{1,0:T(8,128)(2,1)} %bitcast.14, bf16[256,128]{1,0:T(8,128)(2,1)S(1)} %reshape.30), kind=kLoop, calls=%fused_computation | loop fusion | flops 442368 | bytes 294912 | tf_op jit(solution)/shard_map/concatenate | solution.py:313
  4.1 0.0 copy-start
  4.1 0.7 copy-done
  4.8 0.0 copy-start.1
  4.8 0.7 copy-done.1
  5.5 65.7 %fused.1 = f32[2,64,128]{2,1,0:T(8,128)S(1)} custom-call(s32[8,32]{1,0:T(8,128)S(1)} %copy-done.1, bf16[512,16,512]{2,1,0:T(8,128)(2,1)} %screened.1, bf16[576,128]{1,0:T(8,128)(2,1)S(1)} %pad_maximum_fusion.block, bf16[8,16,128]{2,1,0:T(8,128)(2,1)S(1)} %reshape.34.vsx, bf16[64,64]{1,0:T(8,128)(2,1)S(1)} %bitcast.11), custom_call_target="tpu_custom_call" | custom-call | tf_op jit(solution)/shard_map/fused/pallas_call | solution.py:319
  71.2 0.1 reshape.36
  71.4 0.2 slice_reduce_fusion.1
  71.6 0.1 stack.7
  71.6 0.1 stack.8
  71.7 0.6 pad_maximum_fusion.1
Async XLA Ops:
  4.1 0.7 copy-start
  4.8 0.7 copy-start.1

commit v3 on v2

--- a/solution.py
+++ b/solution.py
@@ -230,13 +230,16 @@
         arrived(vsg.at[speer[ns - j]], vsr.at[j])
     load.wait()
     compute(k, True)
-    for place in range(2, nz):
+    passed(0)
+    compute(kp)
+    relay(order[2])
+    corner(order[1])
+    for place in range(3, nz):
         relay(order[place])
-        corner(order[place - 1])
-        if place == 2:
-            passed(0)
-            compute(kp)
     compute(kx)
+    for place in range(2, nz - 1):
+        corner(order[place])
+    compute(ky)
     corner(order[-1])
     passed(1)
     passed(2)
@@ -249,7 +252,7 @@
         compute(lax.rem(kc + sx * (2 - 4 * side) + 4 * sy, ns))
         return carry
 
-    lax.fori_loop(0, 4, later, 0)
+    lax.fori_loop(1, 4, later, 0)
     passed(3)
     compute(other[3])
 
@@ -350,7 +353,7 @@
     nt, nvec, nc = val_target.shape[0] // nz, trial_vectors.shape[1], cond_target.shape[1]
     rows = aux // (nz * ns)
     return (
-        ns == 8 and nz >= 3 and nt == 2 and 2 * nc == 128 and aux // nz == 128 and rows == 16
+        ns == 8 and nz >= 4 and nt == 2 and 2 * nc == 128 and aux // nz == 128 and rows == 16
         and nvec % (2 * nz) == 0 and nvec % ns == 0 and pair_momentum.size <= 256
     )
 

time: 72.8 us -> 71.1 us (0.977)
  Pallas kernels: 65.7 us -> 64.1 us
    pallas_call x1, Pallas kernels: 65.7 us -> 64.1 us  [local(): pl.pallas_call(functools.partial(fused_kernel, nz, ns, nt, nsl), out_shap...]
where the time goes in v3:
time: 71.1 us; the launch traced here: 70.7 us
  Pallas kernels  64.1 us (90%)
  local copies, waits for them, and re-layouts  5.05 us (7%)
  other arithmetic  1.48 us (2%)
    pallas_call x1, Pallas kernels, local(): pl.pallas_call(functools.partial(fused_kernel, nz, ns, nt, nsl), out_shap...  64.1 us
    unnamed x5, local copies, waits for them, and re-layouts  2.29 us

profile of v3, /device:TPU:0, one launch (start us, length us, event | category | flops | bytes accessed | tf_op | source)
XLA Modules:
  0.0 70.7 jit_solution(10457076896071076660)
XLA Ops:
  0.0 0.8 %copy.15 = bf16[64,128]{1,0:T(8,128)(2,1)S(1)} copy(bf16[64,128]{0,1:T(8,128)(2,1)} %bitcast.15) | data formatting | bytes 32768 | tf_op jit(solution)/shard_map/reshape | solution.py:317
  0.8 0.9 %copy.13 = bf16[4,32,128]{1,2,0:T(8,128)(2,1)S(1)} copy(bf16[4,32,128]{2,1,0:T(8,128)(2,1)} %param.9) | data formatting | bytes 65536 | tf_op args[2]
  1.7 0.1 copy.14
  1.8 0.1 reshape.34.vsx
  2.0 1.0 %reshape.29 = bf16[4,2,2,32,64]{4,3,2,1,0:T(8,128)(2,1)S(1)} reshape(bf16[4,4,2048]{2,1,0:T(4,128)(2,1)} %param.11) | data formatting | bytes 131072 | tf_op jit(solution)/shard_map/reshape | solution.py:315
  3.0 0.1 copy.17
  3.1 0.1 reshape.30
  3.2 0.9 %pad_maximum_fusion.block = bf16[576,128]{1,0:T(8,128)(2,1)S(1)} fusion(bf16[64,128]{1,0:T(8,128)(2,1)S(1)} %copy.15, bf16[256,128]{1,0:T(8,128)(2,1)} %bitcast.14, bf16[256,128]{1,0:T(8,128)(2,1)S(1)} %reshape.30), kind=kLoop, calls=%fused_computation | loop fusion | flops 442368 | bytes 294912 | tf_op jit(solution)/shard_map/concatenate | solution.py:316
  4.1 0.0 copy-start
  4.1 0.7 %copy-done = bf16[2,32,64]{2,1,0:T(8,128)(2,1)S(1)} copy-done((bf16[2,32,64]{2,1,0:T(8,128)(2,1)S(1)}, bf16[2,32,64]{2,1,0:T(8,128)(2,1)}, u32[]{:S(2)}) %copy-start) | copy-done | bytes 8216
  4.8 0.0 copy-start.1
  4.8 0.7 copy-done.1
  5.5 64.1 %fused.1 = f32[2,64,128]{2,1,0:T(8,128)S(1)} custom-call(s32[8,32]{1,0:T(8,128)S(1)} %copy-done.1, bf16[512,16,512]{2,1,0:T(8,128)(2,1)} %screened.1, bf16[576,128]{1,0:T(8,128)(2,1)S(1)} %pad_maximum_fusion.block, bf16[8,16,128]{2,1,0:T(8,128)(2,1)S(1)} %reshape.34.vsx, bf16[64,64]{1,0:T(8,128)(2,1)S(1)} %bitcast.11), custom_call_target="tpu_custom_call" | custom-call | tf_op jit(solution)/shard_map/fused/pallas_call | solution.py:322
  69.5 0.1 reshape.36
  69.7 0.2 slice_reduce_fusion.1
  69.9 0.1 stack.7
  70.0 0.1 stack.8
  70.0 0.6 pad_maximum_fusion.1
Async XLA Ops:
  4.1 0.7 %copy-start = (bf16[2,32,64]{2,1,0:T(8,128)(2,1)S(1)}, bf16[2,32,64]{2,1,0:T(8,128)(2,1)}, u32[]{:S(2)}) copy-start(bf16[2,32,64]{2,1,0:T(8,128)(2,1)} %param.7) | copy-start | bytes 24580
  4.8 0.7 copy-start.1
